TPU v7x, 512 devices: a whole 4x4x16 slice. The times are simulated.
512 devices in a mesh: cube: 16 (over x, z_hi, core), tile: 32 (over y, z_lo).
Axes of the slice: x: 4, y: 4, z: 16 (z_hi: 2, z_lo: 8; z = z_hi * 8 + z_lo), core: 2. Of those that a mesh axis runs over, the one named last changes fastest.
Arguments:
- leaf_fronts: float32 [8, 4096, 1, 8192], P(None, 'cube', None, 'tile'), as said below
- middle_fronts: float32 [4, 4096, 1, 8192], P(None, 'cube', None, 'tile'), as said below
- root_front: float32 [2, 4096, 1, 8192], P(None, 'cube', None, 'tile'), as said below
- leaf_scatter: int32 [4, 32, 256], replicated, may hold values from 0 to 255, each once within a row
- middle_scatter: int32 [2, 32, 256], replicated, may hold values from 0 to 255, each once within a row
- leaf_orders: int32 [4], replicated, may hold values from 4096 to 8192, as said below
- middle_orders: int32 [2], replicated, may hold values from 4096 to 8192, as said below
Outputs:
- leaf_panel: bfloat16 [8, 16, 256, 256], P(None, 'cube', 'tile')
- middle_panel: bfloat16 [4, 16, 256, 256], P(None, 'cube', 'tile')
- root_panel: bfloat16 [2, 16, 256, 256], P(None, 'cube', 'tile')
- root_schur: bfloat16 [2, 4096, 1, 8192], P(None, 'cube', None, 'tile')
Inputs may be any that keep to these rules, and one draw needn't show every extreme that they name: `leaf_fronts`: each front is symmetric and positive definite. `middle_fronts`: each front is symmetric and positive definite. `root_front`: the front is symmetric and positive definite. `leaf_orders`: some front of the level has all 8192 rows live. `middle_orders`: some front of the level has all 8192 rows live.
All inputs are finite; a program needn't handle non-finite values.
Results may differ from a plain program's by a relative error of at most 0.0052.
Values may be sent and summed in bfloat16 or wider, within the bound.
A program may use at most 64 MiB of HBM per device.

v0:
```python
import jax
import jax.numpy as jnp
from jax import lax
from jax.sharding import Mesh
from jax.sharding import PartitionSpec as P

TILE = ("tile_0", "tile_1")


def partner_2(block, axis, apart):
    count = lax.axis_size(axis)
    route = []
    for low in range(count):
        high = low | 1 << apart
        if high != low and high < count:
            route += [(low, high), (high, low)]
    return lax.ppermute(block, axis, route)


def from_root(value, axes, root):
    value = jnp.where(lax.axis_index(axes) == root, value, jnp.zeros_like(value))
    for axis in axes:
        value = lax.psum(value, axis)
    return value


def bit_list(groups):
    levels = groups.bit_length() - 1
    return list(range(levels))


def spread_corner(payload, groups):
    for which_bit in bit_list(groups):
        payload = payload + partner_2(payload, "cube", which_bit)
    return payload


def spread_columns(payload, groups):
    for which_bit in bit_list(groups):
        payload = payload + partner_2(payload, "cube", which_bit)
    return payload


def solve_strip(strip_rows, corner, row_ids, pivot_tile):
    tile_width = strip_rows.shape[1]
    lower_factor = jnp.linalg.cholesky(corner)
    flat_strip = strip_rows.reshape(-1, tile_width)
    solved = jax.scipy.linalg.solve_triangular(lower_factor, flat_strip.T, lower=True).T
    solved = solved.reshape(strip_rows.shape)
    solved = jnp.where((row_ids == pivot_tile)[:, None, None], lower_factor[None], solved)
    return solved.astype(jnp.bfloat16)


def factor_level(front_block, level_depth):
    tile_size = lax.axis_size(TILE)
    groups = lax.axis_size("cube") // 2**level_depth
    pivot_tile = 2 - level_depth
    member = lax.axis_index("cube") % groups
    column_dev = lax.axis_index(TILE)
    tile_rows, tile_width, col_tiles, _ = front_block.shape
    pivot_member = pivot_tile % groups
    pivot_row = pivot_tile // groups
    pivot_dev = pivot_tile % tile_size
    pivot_col = pivot_tile // tile_size
    row_ids = jnp.arange(tile_rows, dtype=jnp.int32) * groups + member
    local_strip = front_block[:, :, pivot_col, :]
    own_column = column_dev == pivot_dev
    corner = jnp.where((member == pivot_member) & own_column, local_strip[pivot_row], 0.0)
    corner = spread_corner(corner, groups)
    identity = jnp.eye(tile_width, dtype=jnp.float32)
    corner = jnp.where(own_column, corner, identity)
    own_rows = solve_strip(local_strip, corner, row_ids, pivot_tile)
    factor_rows = from_root(own_rows, TILE, pivot_dev)
    slice_rows = tile_width // tile_size
    panel_part = lax.dynamic_slice_in_dim(factor_rows, column_dev * slice_rows, slice_rows, 1)
    zeroed = jnp.where(
        (row_ids == pivot_tile)[:, None, None], jnp.zeros_like(factor_rows), factor_rows
    )
    col_ids = jnp.arange(col_tiles, dtype=jnp.int32) * tile_size + column_dev
    picked = jnp.take(zeroed, col_ids // groups, axis=0)
    owned_mask = col_ids % groups == member
    picked = jnp.where(owned_mask[:, None, None], picked, jnp.zeros_like(picked))
    col_factor = spread_columns(picked, groups)
    update = jnp.einsum("rik,cjk->ricj", zeroed, col_factor, preferred_element_type=jnp.float32)
    return (panel_part[:, None], front_block - update)


def permute_tiles(block, row_ids, col_ids, perm_table):
    tile_width = block.shape[1]
    slot_ids = jnp.arange(tile_width, dtype=jnp.int32)
    row_perm = jnp.take(perm_table, row_ids, axis=0)
    col_perm = jnp.take(perm_table, col_ids, axis=0)
    row_onehot = (row_perm[:, None, :] == slot_ids[None, :, None]).astype(jnp.float32)
    col_onehot = (col_perm[:, None, :] == slot_ids[None, :, None]).astype(jnp.float32)
    placed = jnp.einsum("rji,ricy->rjcy", row_onehot, block, precision=lax.Precision.HIGHEST)
    return jnp.einsum("rjcy,cly->rjcl", placed, col_onehot, precision=lax.Precision.HIGHEST)


def send_up(schur_block, level_depth, order_table, scatter_table):
    tile_size = lax.axis_size(TILE)
    groups = lax.axis_size("cube") // 2**level_depth
    pivot_tile = 2 - level_depth
    cube_index = lax.axis_index("cube")
    front_id = cube_index // groups
    member = cube_index % groups
    column_dev = lax.axis_index(TILE)
    tile_rows, tile_width, col_tiles, _ = schur_block.shape
    row_ids = jnp.arange(tile_rows, dtype=jnp.int32) * groups + member
    col_ids = jnp.arange(col_tiles, dtype=jnp.int32) * tile_size + column_dev
    offsets = jnp.arange(tile_width, dtype=jnp.int32)
    live_order = order_table[front_id]
    row_keep = (row_ids[:, None] * tile_width + offsets[None, :] < live_order) & (
        row_ids[:, None] != pivot_tile
    )
    col_keep = (col_ids[:, None] * tile_width + offsets[None, :] < live_order) & (
        col_ids[:, None] != pivot_tile
    )
    keep_both = row_keep[:, :, None, None] & col_keep[None, None, :, :]
    masked = jnp.where(keep_both, schur_block, 0.0)
    parity = front_id % 2
    which_bit = groups.bit_length() - 1
    pair_shape = (tile_rows // 2, 2, tile_width, col_tiles, tile_width)
    tile_pairs = masked.reshape(pair_shape)
    kept_half = jnp.where(parity == 0, tile_pairs[:, 0], tile_pairs[:, 1])
    sent_half = jnp.where(parity == 0, tile_pairs[:, 1], tile_pairs[:, 0])
    received = partner_2(sent_half, "cube", which_bit)
    kept_ids = (jnp.arange(tile_rows // 2, dtype=jnp.int32) * 2 + parity) * groups + member
    partner = front_id + 1 - 2 * parity
    own_part = permute_tiles(kept_half, kept_ids, col_ids, scatter_table[front_id])
    other_part = permute_tiles(received, kept_ids, col_ids, scatter_table[partner])
    return own_part + other_part


def per_device(
    leaf_fronts, middle_fronts, root_front, leaf_scatter, middle_scatter, leaf_orders, middle_orders
):
    leaf_panel, leaf_schur = factor_level(leaf_fronts, 2)
    middle_input = middle_fronts + send_up(leaf_schur, 2, leaf_orders, leaf_scatter)
    middle_panel, middle_schur = factor_level(middle_input, 1)
    root_input = root_front + send_up(middle_schur, 1, middle_orders, middle_scatter)
    root_panel, root_schur = factor_level(root_input, 0)
    return (leaf_panel, middle_panel, root_panel, root_schur.astype(jnp.bfloat16))


def solution(mesh):
    split = Mesh(mesh.devices.reshape(mesh.shape["cube"], 4, 8), ("cube", "tile_0", "tile_1"))
    placed = (
        P(None, "cube", None, TILE),
        P(None, "cube", None, TILE),
        P(None, "cube", None, TILE),
        P(),
        P(),
        P(),
        P(),
    )
    return jax.shard_map(
        per_device,
        mesh=split,
        in_specs=placed,
        out_specs=(
            P(None, "cube", TILE, None),
            P(None, "cube", TILE, None),
            P(None, "cube", TILE, None),
            P(None, "cube", None, TILE),
        ),
        check_vma=False,
    )
```

profile of v0, /device:TPU:12, one launch (start us, length us, event | category | flops | bytes accessed | tf_op | source)
XLA Modules:
  0.0 1045.2 jit_solution(14356378276181455765)
XLA Ops:
  12.2 15.7 %collective-permute-start.1 = (f32[256,256]{0,1:T(8,128)S(1)}, f32[256,256]{0,1:T(8,128)S(1)}, u32[]{:S(2)}, u32[]{:S(2)}) collective-permute-start(f32[256,256]{0,1:T(8,128)S(1)} %fusion.113), channel_id=1, source_target_pairs={{0,64},{64,0},{32,96},{96,32},{128,192},{192,128},{160,224},{224,1... | collective-permute-start | bytes 786440 | tf_op jit(solution)/shard_map/ppermute | solution.py:17
  29.5 5.3 collective-permute-done.1
  35.0 11.7 %cholesky.172 = f32[128,128]{1,0:T(8,128)S(1)} custom-call(f32[128,128]{1,0:T(8,128)S(1)} %cholesky.270), custom_call_target="Cholesky" | custom-call | tf_op jit(solution)/shard_map/jit(cholesky)/cholesky | solution.py:46
  46.8 9.8 custom-call.25
  57.1 11.7 %cholesky.189 = f32[128,128]{1,0:T(8,128)S(1)} custom-call(f32[128,128]{1,0:T(8,128)S(1)} %convolution_subtract_fusion.5), custom_call_target="Cholesky" | custom-call | tf_op jit(solution)/shard_map/jit(cholesky)/cholesky | solution.py:46
  75.1 19.7 %custom-call.20 = f32[2,128,128]{1,2,0:T(8,128)S(1)} custom-call(f32[2,128,128]{2,1,0:T(8,128)S(1)} %get-tuple-element.23), custom_call_target="InvertDiagBlocksLowerTriangular" | custom-call | tf_op jit(solution)/shard_map/jit(_solve_triangular)/triangular_solve | solution.py:48
  100.6 78.1 %all-reduce.8.cloned.1.call-done = bf16[8,256,256]{2,1,0:T(8,128)(2,1)} async-done(((bf16[8,256,256]{2,1,0:T(8,128)(2,1)}), bf16[8,256,256]{2,1,0:T(8,128)(2,1)}) %all-reduce.8.cloned.1.call-update) | async-done | bytes 1048592 | tf_op jit(solution)/shard_map/psum | solution.py:23
  179.4 132.8 %all-reduce.10.cloned.1.call-done = bf16[8,256,256]{2,1,0:T(8,128)(2,1)} async-done(((bf16[8,256,256]{2,1,0:T(8,128)(2,1)}), bf16[8,256,256]{2,1,0:T(8,128)(2,1)}) %all-reduce.10.cloned.1.call-update) | async-done | bytes 1048592 | tf_op jit(solution)/shard_map/psum | solution.py:23
  322.7 11.3 %collective-permute-done.3 = bf16[1,256,256]{2,1,0:T(8,128)(2,1)S(1)} collective-permute-done((bf16[1,256,256]{2,1,0:T(8,128)(2,1)S(1)}, bf16[1,256,256]{2,1,0:T(8,128)(2,1)S(1)}, u32[]{:S(2)}, u32[]{:S(2)}) %collective-permute-start.3) | collective-permute-done | bytes 131104 | tf_op jit(solution)/shard_map/ppermute | solution.py:17
  345.6 19.1 %collective-permute-done.4 = f32[4,256,1,256]{3,1,0,2:T(8,128)} collective-permute-done((f32[4,256,1,256]{3,1,0,2:T(8,128)}, f32[4,256,1,256]{3,1,0,2:T(8,128)}, u32[]{:S(2)}, u32[]{:S(2)}) %collective-permute-start.4) | collective-permute-done | bytes 1048608 | tf_op jit(solution)/shard_map/ppermute | solution.py:17
  370.9 9.2 collective-permute-start.6
  380.1 15.8 %collective-permute-done.6 = f32[256,256]{0,1:T(8,128)S(1)} collective-permute-done((f32[256,256]{0,1:T(8,128)S(1)}, f32[256,256]{0,1:T(8,128)S(1)}, u32[]{:S(2)}, u32[]{:S(2)}) %collective-permute-start.6) | collective-permute-done | bytes 262176 | tf_op jit(solution)/shard_map/ppermute | solution.py:17
  399.5 6.4 collective-permute-done.7
  406.2 11.7 %cholesky.206 = f32[128,128]{1,0:T(8,128)S(1)} custom-call(f32[128,128]{1,0:T(8,128)S(1)} %cholesky.273), custom_call_target="Cholesky" | custom-call | tf_op jit(solution)/shard_map/jit(cholesky)/cholesky | solution.py:46
  418.0 9.8 custom-call.26
  428.3 11.7 %cholesky.223 = f32[128,128]{1,0:T(8,128)S(1)} custom-call(f32[128,128]{1,0:T(8,128)S(1)} %convolution_subtract_fusion.4), custom_call_target="Cholesky" | custom-call | tf_op jit(solution)/shard_map/jit(cholesky)/cholesky | solution.py:46
  447.2 19.7 %custom-call.21 = f32[2,128,128]{1,2,0:T(8,128)S(1)} custom-call(f32[2,128,128]{2,1,0:T(8,128)S(1)} %get-tuple-element.39), custom_call_target="InvertDiagBlocksLowerTriangular" | custom-call | tf_op jit(solution)/shard_map/jit(_solve_triangular)/triangular_solve | solution.py:48
  470.6 57.2 %all-reduce.12.cloned.1.call-done = bf16[4,256,256]{2,1,0:T(8,128)(2,1)} async-done(((bf16[4,256,256]{2,1,0:T(8,128)(2,1)}), bf16[4,256,256]{2,1,0:T(8,128)(2,1)}) %all-reduce.12.cloned.1.call-update) | async-done | bytes 524304 | tf_op jit(solution)/shard_map/psum | solution.py:23
  529.1 126.9 %all-reduce.14.cloned.1.call-done = bf16[4,256,256]{2,1,0:T(8,128)(2,1)} async-done(((bf16[4,256,256]{2,1,0:T(8,128)(2,1)}), bf16[4,256,256]{2,1,0:T(8,128)(2,1)}) %all-reduce.14.cloned.1.call-update) | async-done | bytes 524304 | tf_op jit(solution)/shard_map/psum | solution.py:23
  666.4 11.7 %collective-permute-done.9 = bf16[1,256,256]{2,1,0:T(8,128)(2,1)S(1)} collective-permute-done((bf16[1,256,256]{2,1,0:T(8,128)(2,1)S(1)}, bf16[1,256,256]{2,1,0:T(8,128)(2,1)S(1)}, u32[]{:S(2)}, u32[]{:S(2)}) %collective-permute-start.9) | collective-permute-done | bytes 131104 | tf_op jit(solution)/shard_map/ppermute | solution.py:17
  690.5 12.8 %collective-permute-done.11 = f32[2,256,1,256]{1,3,0,2:T(8,128)S(1)} collective-permute-done((f32[2,256,1,256]{1,3,0,2:T(8,128)}, f32[2,256,1,256]{1,3,0,2:T(8,128)S(1)}, u32[]{:S(2)}, u32[]{:S(2)}) %collective-permute-start.11) | collective-permute-done | bytes 524320 | tf_op jit(solution)/shard_map/ppermute | solution.py:17
  707.8 8.0 collective-permute-start.13
  715.7 16.6 %collective-permute-done.13 = f32[256,256]{0,1:T(8,128)S(1)} collective-permute-done((f32[256,256]{0,1:T(8,128)S(1)}, f32[256,256]{0,1:T(8,128)S(1)}, u32[]{:S(2)}, u32[]{:S(2)}) %collective-permute-start.13) | collective-permute-done | bytes 262176 | tf_op jit(solution)/shard_map/ppermute | solution.py:17
  735.5 7.1 collective-permute-done.14
  745.4 7.9 collective-permute-done.15
  753.6 11.7 %cholesky.240 = f32[128,128]{1,0:T(8,128)S(1)} custom-call(f32[128,128]{1,0:T(8,128)S(1)} %cholesky.276), custom_call_target="Cholesky" | custom-call | tf_op jit(solution)/shard_map/jit(cholesky)/cholesky | solution.py:46
  765.4 9.8 custom-call.27
  775.7 11.7 %cholesky.257 = f32[128,128]{1,0:T(8,128)S(1)} custom-call(f32[128,128]{1,0:T(8,128)S(1)} %convolution_subtract_fusion.3), custom_call_target="Cholesky" | custom-call | tf_op jit(solution)/shard_map/jit(cholesky)/cholesky | solution.py:46
  794.5 19.7 %custom-call.22 = f32[2,128,128]{1,2,0:T(8,128)S(1)} custom-call(f32[2,128,128]{2,1,0:T(8,128)S(1)} %get-tuple-element.55), custom_call_target="InvertDiagBlocksLowerTriangular" | custom-call | tf_op jit(solution)/shard_map/jit(_solve_triangular)/triangular_solve | solution.py:48
  816.6 55.5 %all-reduce.16.cloned.1.call-done = bf16[2,256,256]{2,1,0:T(8,128)(2,1)} async-done(((bf16[2,256,256]{2,1,0:T(8,128)(2,1)}), bf16[2,256,256]{2,1,0:T(8,128)(2,1)}) %all-reduce.16.cloned.1.call-update) | async-done | bytes 262160 | tf_op jit(solution)/shard_map/psum | solution.py:23
  872.2 126.7 %all-reduce.18.cloned.1.call-done = bf16[2,256,256]{2,1,0:T(8,128)(2,1)} async-done(((bf16[2,256,256]{2,1,0:T(8,128)(2,1)}), bf16[2,256,256]{2,1,0:T(8,128)(2,1)}) %all-reduce.18.cloned.1.call-update) | async-done | bytes 262160 | tf_op jit(solution)/shard_map/psum | solution.py:23
  1008.6 12.6 %collective-permute-done.17 = bf16[1,256,256]{2,1,0:T(8,128)(2,1)S(1)} collective-permute-done((bf16[1,256,256]{2,1,0:T(8,128)(2,1)S(1)}, bf16[1,256,256]{2,1,0:T(8,128)(2,1)S(1)}, u32[]{:S(2)}, u32[]{:S(2)}) %collective-permute-start.17) | collective-permute-done | bytes 131104 | tf_op jit(solution)/shard_map/ppermute | solution.py:17
  (205 shorter events, 142.3 us)
Async XLA Ops:
  7.2 20.7 %copy-start = (f32[8,256,1,256]{3,2,1,0:T(1,128)S(1)}, f32[8,256,1,256]{3,2,1,0:T(1,128)}, u32[]{:S(2)}) copy-start(f32[8,256,1,256]{3,2,1,0:T(1,128)} %param.14) | copy-start | bytes 6291460
  7.2 171.5 %all-reduce.8.cloned.1.call-start = ((), (), s32[]{:S(2)}) async-start(), calls=%async_computation | async-start | bytes 2097152 | tf_op jit(solution)/shard_map/psum | solution.py:23
  8.7 3.4 collective-permute-start
  12.2 22.6 %collective-permute-start.1 = (f32[256,256]{0,1:T(8,128)S(1)}, f32[256,256]{0,1:T(8,128)S(1)}, u32[]{:S(2)}, u32[]{:S(2)}) collective-permute-start(f32[256,256]{0,1:T(8,128)S(1)} %fusion.113), channel_id=1, source_target_pairs={{0,64},{64,0},{32,96},{96,32},{128,192},{192,128},{160,224},{224,1... | collective-permute-start | bytes 786440 | tf_op jit(solution)/shard_map/ppermute | solution.py:17
  34.8 59.9 %copy-start.1 = (f32[8,256,1,256]{3,1,2,0:T(8,128)S(1)}, f32[8,256,1,256]{3,1,2,0:T(8,128)}, u32[]{:S(2)}) copy-start(f32[8,256,1,256]{3,1,2,0:T(8,128)} %copy.56) | copy-start | bytes 6291460
  99.4 79.4 %copy-start.5 = (s32[4]{0:T(128)S(1)}, s32[4]{0:T(128)}, u32[]{:S(2)}) copy-start(s32[4]{0:T(128)} %param.19) | copy-start | bytes 52
  100.6 222.1 %copy-start.4 = (s32[4,32,256]{2,1,0:T(8,128)S(1)}, s32[4,32,256]{2,1,0:T(8,128)}, u32[]{:S(2)}) copy-start(s32[4,32,256]{2,1,0:T(8,128)} %param.17) | copy-start | bytes 393220
  100.6 211.6 %all-reduce.10.cloned.1.call-start = ((), (), s32[]{:S(2)}) async-start(), calls=%async_computation.1 | async-start | bytes 2097152 | tf_op jit(solution)/shard_map/psum | solution.py:23
  178.7 349.0 %all-reduce.12.cloned.1.call-start = ((), (), s32[]{:S(2)}) async-start(), calls=%async_computation.2 | async-start | bytes 1048576 | tf_op jit(solution)/shard_map/psum | solution.py:23
  313.6 3.2 collective-permute-start.2
  316.8 17.1 %collective-permute-start.3 = (bf16[1,256,256]{2,1,0:T(8,128)(2,1)S(1)}, bf16[1,256,256]{2,1,0:T(8,128)(2,1)S(1)}, u32[]{:S(2)}, u32[]{:S(2)}) collective-permute-start(bf16[1,256,256]{2,1,0:T(8,128)(2,1)S(1)} %fusion.112), channel_id=1, source_target_pairs={{0,64},{64,0},{32,96},{96,32},{128,192},{192,128},{160,224},{224,1... | collective-permute-start | bytes 393224 | tf_op jit(solution)/shard_map/ppermute | solution.py:17
  337.4 27.3 %collective-permute-start.4 = (f32[4,256,1,256]{3,1,0,2:T(8,128)}, f32[4,256,1,256]{3,1,0,2:T(8,128)}, u32[]{:S(2)}, u32[]{:S(2)}) collective-permute-start(f32[4,256,1,256]{3,1,0,2:T(8,128)} %select_bitcast_fusion), channel_id=1, source_target_pairs={{0,128},{128,0},{32,160},{160,32},{64,192},{192,64},{96,224},{224,... | collective-permute-start | bytes 3145736 | tf_op jit(solution)/shard_map/ppermute | solution.py:17
  367.4 3.4 collective-permute-start.5
  370.9 24.9 %collective-permute-start.6 = (f32[256,256]{0,1:T(8,128)S(1)}, f32[256,256]{0,1:T(8,128)S(1)}, u32[]{:S(2)}, u32[]{:S(2)}) collective-permute-start(f32[256,256]{0,1:T(8,128)S(1)} %fusion.111), channel_id=1, source_target_pairs={{0,64},{64,0},{32,96},{96,32},{128,192},{192,128},{160,224},{224,1... | collective-permute-start | bytes 786440 | tf_op jit(solution)/shard_map/ppermute | solution.py:17
  395.9 10.1 collective-permute-start.7
  469.2 58.7 %copy-start.3 = (s32[2,32,256]{2,1,0:T(8,128)S(1)}, s32[2,32,256]{2,1,0:T(8,128)}, u32[]{:S(2)}) copy-start(s32[2,32,256]{2,1,0:T(8,128)} %param.18) | copy-start | bytes 196612
  469.5 189.7 %copy-start.6 = (s32[2]{0:T(128)S(1)}, s32[2]{0:T(128)}, u32[]{:S(2)}) copy-start(s32[2]{0:T(128)} %param.20) | copy-start | bytes 28
  470.4 185.6 %all-reduce.14.cloned.1.call-start = ((), (), s32[]{:S(2)}) async-start(), calls=%async_computation.3 | async-start | bytes 1048576 | tf_op jit(solution)/shard_map/psum | solution.py:23
  527.8 344.4 %all-reduce.16.cloned.1.call-start = ((), (), s32[]{:S(2)}) async-start(), calls=%async_computation.4 | async-start | bytes 524288 | tf_op jit(solution)/shard_map/psum | solution.py:23
  657.2 3.2 collective-permute-start.8
  660.5 17.6 %collective-permute-start.9 = (bf16[1,256,256]{2,1,0:T(8,128)(2,1)S(1)}, bf16[1,256,256]{2,1,0:T(8,128)(2,1)S(1)}, u32[]{:S(2)}, u32[]{:S(2)}) collective-permute-start(bf16[1,256,256]{2,1,0:T(8,128)(2,1)S(1)} %fusion.110), channel_id=1, source_target_pairs={{0,64},{64,0},{32,96},{96,32},{128,192},{192,128},{160,224},{224,1... | collective-permute-start | bytes 393224 | tf_op jit(solution)/shard_map/ppermute | solution.py:17
  678.1 7.3 collective-permute-start.10
  686.7 16.6 %collective-permute-start.11 = (f32[2,256,1,256]{1,3,0,2:T(8,128)}, f32[2,256,1,256]{1,3,0,2:T(8,128)S(1)}, u32[]{:S(2)}, u32[]{:S(2)}) collective-permute-start(f32[2,256,1,256]{1,3,0,2:T(8,128)} %select_bitcast_fusion.1), channel_id=1, source_target_pairs={{0,256},{256,0},{32,288},{288,32},{64,320},{320,64},{96,352},{352,... | collective-permute-start | bytes 1572872 | tf_op jit(solution)/shard_map/ppermute | solution.py:17
  704.3 3.4 collective-permute-start.12
  707.8 24.6 %collective-permute-start.13 = (f32[256,256]{0,1:T(8,128)S(1)}, f32[256,256]{0,1:T(8,128)S(1)}, u32[]{:S(2)}, u32[]{:S(2)}) collective-permute-start(f32[256,256]{0,1:T(8,128)S(1)} %fusion.109), channel_id=1, source_target_pairs={{0,64},{64,0},{32,96},{96,32},{128,192},{192,128},{160,224},{224,1... | collective-permute-start | bytes 786440 | tf_op jit(solution)/shard_map/ppermute | solution.py:17
  732.4 10.1 collective-permute-start.14
  742.6 10.8 %collective-permute-start.15 = (f32[256,256]{0,1:T(8,128)S(1)}, f32[256,256]{0,1:T(8,128)S(1)}, u32[]{:S(2)}, u32[]{:S(2)}) collective-permute-start(f32[256,256]{0,1:T(8,128)S(1)} %add.403), channel_id=1, source_target_pairs={{0,256},{256,0},{32,288},{288,32},{64,320},{320,64},{96,352},{352,... | collective-permute-start | bytes 786440 | tf_op jit(solution)/shard_map/ppermute | solution.py:17
  816.6 182.3 %all-reduce.18.cloned.1.call-start = ((), (), s32[]{:S(2)}) async-start(), calls=%async_computation.5 | async-start | bytes 524288 | tf_op jit(solution)/shard_map/psum | solution.py:23
  1000.0 3.2 collective-permute-start.16
  1003.3 17.9 %collective-permute-start.17 = (bf16[1,256,256]{2,1,0:T(8,128)(2,1)S(1)}, bf16[1,256,256]{2,1,0:T(8,128)(2,1)S(1)}, u32[]{:S(2)}, u32[]{:S(2)}) collective-permute-start(bf16[1,256,256]{2,1,0:T(8,128)(2,1)S(1)} %fusion.108), channel_id=1, source_target_pairs={{0,64},{64,0},{32,96},{96,32},{128,192},{192,128},{160,224},{224,1... | collective-permute-start | bytes 393224 | tf_op jit(solution)/shard_map/ppermute | solution.py:17
  1021.2 7.3 collective-permute-start.18
  1028.6 8.4 collective-permute-start.19
  (1 other events, 7.3 us)
Sparse Core Ops, SparseCore 0:
  100.7 77.9 all-reduce.7
  181.6 130.5 all-reduce.9
  470.6 57.1 all-reduce.11
  530.5 125.4 all-reduce.13
  816.7 55.4 all-reduce.15
  874.9 123.9 all-reduce.17
where the time goes:
time: 1050 us
  waiting for transfers between devices  721 us (69%)
  other arithmetic  175 us (17%)
  starting transfers between devices  83.2 us (8%)
  local copies, waits for them, and re-layouts  27.9 us (3%)
  between operations  19.5 us (2%)
  matrix products  18 us (2%)
    psum x6, waiting for transfers between devices, from_root(): value = lax.psum(value, axis)  577 us
    ppermute x20, waiting for transfers between devices, partner_2(): return lax.ppermute(block, axis, route)  143 us
    another operation x20, other arithmetic, solve_strip(): lower_factor = jnp.linalg.cholesky(corner)  103 us
    ppermute x20, starting transfers between devices, partner_2(): return lax.ppermute(block, axis, route)  83 us
    another operation x7, other arithmetic, solve_strip(): jax.scipy.linalg.solve_triangular(lower_factor, flat_strip.T, lower=True)  59.1 us
  transfers between devices with their start and end apart: 26, of which 26 were waited for; matrix products, arithmetic and copies ran while one was open for 2% of the time, Pallas kernels for 0%

commit v1 on v0

--- a/solution.py
+++ b/solution.py
@@ -20,7 +20,7 @@
 def from_root(value, axes, root):
     value = jnp.where(lax.axis_index(axes) == root, value, jnp.zeros_like(value))
     for axis in axes:
-        value = lax.psum(value, axis)
+        value = jnp.sum(lax.all_gather(value, axis), axis=0)
     return value
 
 

time: 1050 us -> 1010 us (0.962)
  the two profiles are of different devices: /device:TPU:12 before, /device:TPU:4 now
where the time goes in v1:
time: 1010 us; the launch traced here: 997 us
  waiting for transfers between devices  656 us (65%)
  other arithmetic  192 us (19%)
  starting transfers between devices  83.1 us (8%)
  local copies, waits for them, and re-layouts  28.8 us (3%)
  between operations  19.5 us (2%)
  matrix products  17.5 us (2%)
    all_gather x6, waiting for transfers between devices, from_root(): value = jnp.sum(lax.all_gather(value, axis), axis=0)  496 us
    ppermute x20, waiting for transfers between devices, partner_2(): return lax.ppermute(block, axis, route)  160 us
    another operation x20, other arithmetic, solve_strip(): lower_factor = jnp.linalg.cholesky(corner)  103 us
    ppermute x20, starting transfers between devices, partner_2(): return lax.ppermute(block, axis, route)  82.8 us
    another operation x7, other arithmetic, solve_strip(): jax.scipy.linalg.solve_triangular(lower_factor, flat_strip.T, lower=True)  59.3 us
  transfers between devices with their start and end apart: 26, of which 26 were waited for; matrix products, arithmetic and copies ran while one was open for 2% of the time, Pallas kernels for 0%

profile of v1, /device:TPU:4, one launch (start us, length us, event | category | flops | bytes accessed | tf_op | source)
XLA Modules:
  0.0 997.2 jit_solution(7111754305175341370)
XLA Ops:
  12.2 15.7 %collective-permute-start.1 = (f32[256,256]{0,1:T(8,128)S(1)}, f32[256,256]{0,1:T(8,128)S(1)}, u32[]{:S(2)}, u32[]{:S(2)}) collective-permute-start(f32[256,256]{0,1:T(8,128)S(1)} %fusion.110), channel_id=1, source_target_pairs={{0,64},{64,0},{32,96},{96,32},{128,192},{192,128},{160,224},{224,1... | collective-permute-start | bytes 786440 | tf_op jit(solution)/shard_map/ppermute | solution.py:17
  35.0 11.7 %cholesky.172 = f32[128,128]{1,0:T(8,128)S(1)} custom-call(f32[128,128]{1,0:T(8,128)S(1)} %cholesky.270), custom_call_target="Cholesky" | custom-call | tf_op jit(solution)/shard_map/jit(cholesky)/cholesky | solution.py:46
  46.8 9.8 custom-call.25
  57.1 11.7 %cholesky.189 = f32[128,128]{1,0:T(8,128)S(1)} custom-call(f32[128,128]{1,0:T(8,128)S(1)} %convolution_subtract_fusion.5), custom_call_target="Cholesky" | custom-call | tf_op jit(solution)/shard_map/jit(cholesky)/cholesky | solution.py:46
  74.6 19.9 %custom-call.20 = f32[2,128,128]{1,2,0:T(8,128)S(1)} custom-call(f32[2,128,128]{2,1,0:T(8,128)S(1)} %get-tuple-element.23), custom_call_target="InvertDiagBlocksLowerTriangular" | custom-call | tf_op jit(solution)/shard_map/jit(_solve_triangular)/triangular_solve | solution.py:48
  99.5 73.2 %all-gather.10.cloned.1.call-done = bf16[4,8,256,256]{3,2,1,0:T(8,128)(2,1)} async-done(((bf16[1,8,256,256]{3,2,1,0:T(8,128)(2,1)}), bf16[4,8,256,256]{3,2,1,0:T(8,128)(2,1)}) %all-gather.10.cloned.1.call-update) | async-done | bytes 4194320 | tf_op jit(solution)/shard_map/all_gather | solution.py:23
  177.7 181.8 %all-gather.16.cloned.1.call-done = bf16[64,256,256]{2,1,0:T(8,128)(2,1)} async-done(((bf16[8,256,256]{2,1,0:T(8,128)(2,1)}), bf16[64,256,256]{2,1,0:T(8,128)(2,1)}) %all-gather.16.cloned.1.call-update) | async-done | bytes 8388624 | tf_op jit(solution)/shard_map/all_gather | solution.py:23
  368.1 6.0 collective-permute-start.3
  374.8 16.5 %collective-permute-done.3 = bf16[1,256,256]{2,1,0:T(8,128)(2,1)S(1)} collective-permute-done((bf16[1,256,256]{2,1,0:T(8,128)(2,1)S(1)}, bf16[1,256,256]{2,1,0:T(8,128)(2,1)S(1)}, u32[]{:S(2)}, u32[]{:S(2)}) %collective-permute-start.3) | collective-permute-done | bytes 131104 | tf_op jit(solution)/shard_map/ppermute | solution.py:17
  402.9 19.0 %collective-permute-done.4 = f32[4,256,1,256]{3,1,0,2:T(8,128)} collective-permute-done((f32[4,256,1,256]{3,1,0,2:T(8,128)}, f32[4,256,1,256]{3,1,0,2:T(8,128)}, u32[]{:S(2)}, u32[]{:S(2)}) %collective-permute-start.4) | collective-permute-done | bytes 1048608 | tf_op jit(solution)/shard_map/ppermute | solution.py:17
  433.3 22.0 %collective-permute-done.6 = f32[256,256]{0,1:T(8,128)S(1)} collective-permute-done((f32[256,256]{0,1:T(8,128)S(1)}, f32[256,256]{0,1:T(8,128)S(1)}, u32[]{:S(2)}, u32[]{:S(2)}) %collective-permute-start.6) | collective-permute-done | bytes 262176 | tf_op jit(solution)/shard_map/ppermute | solution.py:17
  459.5 6.1 collective-permute-done.7
  466.8 11.7 %cholesky.206 = f32[128,128]{1,0:T(8,128)S(1)} custom-call(f32[128,128]{1,0:T(8,128)S(1)} %cholesky.273), custom_call_target="Cholesky" | custom-call | tf_op jit(solution)/shard_map/jit(cholesky)/cholesky | solution.py:46
  478.5 9.8 custom-call.26
  488.8 11.7 %cholesky.223 = f32[128,128]{1,0:T(8,128)S(1)} custom-call(f32[128,128]{1,0:T(8,128)S(1)} %convolution_subtract_fusion.4), custom_call_target="Cholesky" | custom-call | tf_op jit(solution)/shard_map/jit(cholesky)/cholesky | solution.py:46
  507.3 19.7 %custom-call.21 = f32[2,128,128]{1,2,0:T(8,128)S(1)} custom-call(f32[2,128,128]{2,1,0:T(8,128)S(1)} %get-tuple-element.39), custom_call_target="InvertDiagBlocksLowerTriangular" | custom-call | tf_op jit(solution)/shard_map/jit(_solve_triangular)/triangular_solve | solution.py:48
  530.2 36.4 %all-gather.12.cloned.1.call-done = bf16[4,4,256,256]{3,2,1,0:T(8,128)(2,1)} async-done(((bf16[1,4,256,256]{3,2,1,0:T(8,128)(2,1)}), bf16[4,4,256,256]{3,2,1,0:T(8,128)(2,1)}) %all-gather.12.cloned.1.call-update) | async-done | bytes 2097168 | tf_op jit(solution)/shard_map/all_gather | solution.py:23
  570.8 102.4 %all-gather.18.cloned.1.call-done = bf16[32,256,256]{2,1,0:T(8,128)(2,1)} async-done(((bf16[4,256,256]{2,1,0:T(8,128)(2,1)}), bf16[32,256,256]{2,1,0:T(8,128)(2,1)}) %all-gather.18.cloned.1.call-update) | async-done | bytes 4194320 | tf_op jit(solution)/shard_map/all_gather | solution.py:23
  686.0 15.4 %collective-permute-done.9 = bf16[1,256,256]{2,1,0:T(8,128)(2,1)S(1)} collective-permute-done((bf16[1,256,256]{2,1,0:T(8,128)(2,1)S(1)}, bf16[1,256,256]{2,1,0:T(8,128)(2,1)S(1)}, u32[]{:S(2)}, u32[]{:S(2)}) %collective-permute-start.9) | collective-permute-done | bytes 131104 | tf_op jit(solution)/shard_map/ppermute | solution.py:17
  714.3 12.9 %collective-permute-done.11 = f32[2,256,1,256]{3,1,0,2:T(8,128)} collective-permute-done((f32[2,256,1,256]{3,1,0,2:T(8,128)}, f32[2,256,1,256]{3,1,0,2:T(8,128)}, u32[]{:S(2)}, u32[]{:S(2)}) %collective-permute-start.11) | collective-permute-done | bytes 524320 | tf_op jit(solution)/shard_map/ppermute | solution.py:17
  732.6 7.8 collective-permute-start.13
  740.4 19.6 %collective-permute-done.13 = f32[256,256]{0,1:T(8,128)S(1)} collective-permute-done((f32[256,256]{0,1:T(8,128)S(1)}, f32[256,256]{0,1:T(8,128)S(1)}, u32[]{:S(2)}, u32[]{:S(2)}) %collective-permute-start.13) | collective-permute-done | bytes 262176 | tf_op jit(solution)/shard_map/ppermute | solution.py:17
  763.2 7.0 collective-permute-done.14
  773.4 7.7 collective-permute-done.15
  781.3 11.7 %cholesky.240 = f32[128,128]{1,0:T(8,128)S(1)} custom-call(f32[128,128]{1,0:T(8,128)S(1)} %cholesky.276), custom_call_target="Cholesky" | custom-call | tf_op jit(solution)/shard_map/jit(cholesky)/cholesky | solution.py:46
  793.1 9.8 custom-call.27
  803.4 11.7 %cholesky.257 = f32[128,128]{1,0:T(8,128)S(1)} custom-call(f32[128,128]{1,0:T(8,128)S(1)} %convolution_subtract_fusion.3), custom_call_target="Cholesky" | custom-call | tf_op jit(solution)/shard_map/jit(cholesky)/cholesky | solution.py:46
  821.7 19.7 %custom-call.22 = f32[2,128,128]{1,2,0:T(8,128)S(1)} custom-call(f32[2,128,128]{2,1,0:T(8,128)S(1)} %get-tuple-element.55), custom_call_target="InvertDiagBlocksLowerTriangular" | custom-call | tf_op jit(solution)/shard_map/jit(_solve_triangular)/triangular_solve | solution.py:48
  843.7 30.7 %all-gather.14.cloned.1.call-done = bf16[4,2,256,256]{3,2,1,0:T(8,128)(2,1)} async-done(((bf16[1,2,256,256]{3,2,1,0:T(8,128)(2,1)}), bf16[4,2,256,256]{3,2,1,0:T(8,128)(2,1)}) %all-gather.14.cloned.1.call-update) | async-done | bytes 1048592 | tf_op jit(solution)/shard_map/all_gather | solution.py:23
  876.6 71.0 %all-gather.20.cloned.1.call-done = bf16[16,256,256]{2,1,0:T(8,128)(2,1)} async-done(((bf16[2,256,256]{2,1,0:T(8,128)(2,1)}), bf16[16,256,256]{2,1,0:T(8,128)(2,1)}) %all-gather.20.cloned.1.call-update) | async-done | bytes 2097168 | tf_op jit(solution)/shard_map/all_gather | solution.py:23
  952.9 7.5 collective-permute-start.17
  960.5 12.6 %collective-permute-done.17 = bf16[1,256,256]{2,1,0:T(8,128)(2,1)S(1)} collective-permute-done((bf16[1,256,256]{2,1,0:T(8,128)(2,1)S(1)}, bf16[1,256,256]{2,1,0:T(8,128)(2,1)S(1)}, u32[]{:S(2)}, u32[]{:S(2)}) %collective-permute-start.17) | collective-permute-done | bytes 131104 | tf_op jit(solution)/shard_map/ppermute | solution.py:17
  (217 shorter events, 158.8 us)
Async XLA Ops:
  7.2 20.7 %copy-start = (f32[8,256,1,256]{3,2,1,0:T(1,128)S(1)}, f32[8,256,1,256]{3,2,1,0:T(1,128)}, u32[]{:S(2)}) copy-start(f32[8,256,1,256]{3,2,1,0:T(1,128)} %param.14) | copy-start | bytes 6291460
  7.2 165.5 %all-gather.10.cloned.1.call-start = ((), (), s32[]{:S(2)}) async-start(), calls=%async_computation | async-start | bytes 5242880 | tf_op jit(solution)/shard_map/all_gather | solution.py:23
  8.7 3.4 collective-permute-start
  12.2 22.6 %collective-permute-start.1 = (f32[256,256]{0,1:T(8,128)S(1)}, f32[256,256]{0,1:T(8,128)S(1)}, u32[]{:S(2)}, u32[]{:S(2)}) collective-permute-start(f32[256,256]{0,1:T(8,128)S(1)} %fusion.110), channel_id=1, source_target_pairs={{0,64},{64,0},{32,96},{96,32},{128,192},{192,128},{160,224},{224,1... | collective-permute-start | bytes 786440 | tf_op jit(solution)/shard_map/ppermute | solution.py:17
  99.5 77.6 %copy-start.5 = (s32[4]{0:T(128)S(1)}, s32[4]{0:T(128)}, u32[]{:S(2)}) copy-start(s32[4]{0:T(128)} %param.19) | copy-start | bytes 52
  99.5 260.0 %all-gather.16.cloned.1.call-start = ((), (), s32[]{:S(2)}) async-start(), calls=%async_computation.3 | async-start | bytes 9437184 | tf_op jit(solution)/shard_map/all_gather | solution.py:23
  176.9 389.6 %all-gather.12.cloned.1.call-start = ((), (), s32[]{:S(2)}) async-start(), calls=%async_computation.1 | async-start | bytes 2621440 | tf_op jit(solution)/shard_map/all_gather | solution.py:23
  364.5 10.3 %copy-start.1 = (bf16[8,256,256]{2,1,0:T(8,128)(2,1)}, bf16[8,256,256]{2,1,0:T(8,128)(2,1)S(1)}, u32[]{:S(2)}) copy-start(bf16[8,256,256]{2,1,0:T(8,128)(2,1)S(1)} %reduce_sum.73) | copy-start | bytes 3145732
  364.5 10.2 %copy-start.4 = (s32[4,32,256]{2,1,0:T(8,128)S(1)}, s32[4,32,256]{2,1,0:T(8,128)}, u32[]{:S(2)}) copy-start(s32[4,32,256]{2,1,0:T(8,128)} %param.17) | copy-start | bytes 393220
  364.7 3.4 collective-permute-start.2
  368.1 23.2 %collective-permute-start.3 = (bf16[1,256,256]{2,1,0:T(8,128)(2,1)S(1)}, bf16[1,256,256]{2,1,0:T(8,128)(2,1)S(1)}, u32[]{:S(2)}, u32[]{:S(2)}) collective-permute-start(bf16[1,256,256]{2,1,0:T(8,128)(2,1)S(1)} %fusion.109), channel_id=1, source_target_pairs={{0,64},{64,0},{32,96},{96,32},{128,192},{192,128},{160,224},{224,1... | collective-permute-start | bytes 393224 | tf_op jit(solution)/shard_map/ppermute | solution.py:17
  394.7 27.3 %collective-permute-start.4 = (f32[4,256,1,256]{3,1,0,2:T(8,128)}, f32[4,256,1,256]{3,1,0,2:T(8,128)}, u32[]{:S(2)}, u32[]{:S(2)}) collective-permute-start(f32[4,256,1,256]{3,1,0,2:T(8,128)} %select_bitcast_fusion), channel_id=1, source_target_pairs={{0,128},{128,0},{32,160},{160,32},{64,192},{192,64},{96,224},{224,... | collective-permute-start | bytes 3145736 | tf_op jit(solution)/shard_map/ppermute | solution.py:17
  424.7 3.4 collective-permute-start.5
  428.2 27.1 %collective-permute-start.6 = (f32[256,256]{0,1:T(8,128)S(1)}, f32[256,256]{0,1:T(8,128)S(1)}, u32[]{:S(2)}, u32[]{:S(2)}) collective-permute-start(f32[256,256]{0,1:T(8,128)S(1)} %fusion.108), channel_id=1, source_target_pairs={{0,64},{64,0},{32,96},{96,32},{128,192},{192,128},{160,224},{224,1... | collective-permute-start | bytes 786440 | tf_op jit(solution)/shard_map/ppermute | solution.py:17
  455.3 10.2 %collective-permute-start.7 = (f32[256,256]{0,1:T(8,128)S(1)}, f32[256,256]{0,1:T(8,128)}, u32[]{:S(2)}, u32[]{:S(2)}) collective-permute-start(f32[256,256]{0,1:T(8,128)S(1)} %add.364), channel_id=1, source_target_pairs={{0,128},{128,0},{32,160},{160,32},{64,192},{192,64},{96,224},{224,... | collective-permute-start | bytes 786440 | tf_op jit(solution)/shard_map/ppermute | solution.py:17
  530.1 39.5 %copy-start.3 = (s32[2,32,256]{2,1,0:T(8,128)S(1)}, s32[2,32,256]{2,1,0:T(8,128)}, u32[]{:S(2)}) copy-start(s32[2,32,256]{2,1,0:T(8,128)} %param.18) | copy-start | bytes 196612
  530.1 143.1 %all-gather.18.cloned.1.call-start = ((), (), s32[]{:S(2)}) async-start(), calls=%async_computation.4 | async-start | bytes 4718592 | tf_op jit(solution)/shard_map/all_gather | solution.py:23
  569.5 304.9 %all-gather.14.cloned.1.call-start = ((), (), s32[]{:S(2)}) async-start(), calls=%async_computation.2 | async-start | bytes 1310720 | tf_op jit(solution)/shard_map/all_gather | solution.py:23
  673.3 5.0 copy-start.6
  676.3 3.2 collective-permute-start.8
  679.5 21.9 %collective-permute-start.9 = (bf16[1,256,256]{2,1,0:T(8,128)(2,1)S(1)}, bf16[1,256,256]{2,1,0:T(8,128)(2,1)S(1)}, u32[]{:S(2)}, u32[]{:S(2)}) collective-permute-start(bf16[1,256,256]{2,1,0:T(8,128)(2,1)S(1)} %fusion.107), channel_id=1, source_target_pairs={{0,64},{64,0},{32,96},{96,32},{128,192},{192,128},{160,224},{224,1... | collective-permute-start | bytes 393224 | tf_op jit(solution)/shard_map/ppermute | solution.py:17
  701.4 7.3 collective-permute-start.10
  710.5 16.7 %collective-permute-start.11 = (f32[2,256,1,256]{3,1,0,2:T(8,128)}, f32[2,256,1,256]{3,1,0,2:T(8,128)}, u32[]{:S(2)}, u32[]{:S(2)}) collective-permute-start(f32[2,256,1,256]{3,1,0,2:T(8,128)} %select_bitcast_fusion.1), channel_id=1, source_target_pairs={{0,256},{256,0},{32,288},{288,32},{64,320},{320,64},{96,352},{352,... | collective-permute-start | bytes 1572872 | tf_op jit(solution)/shard_map/ppermute | solution.py:17
  729.2 3.4 collective-permute-start.12
  732.6 27.4 %collective-permute-start.13 = (f32[256,256]{0,1:T(8,128)S(1)}, f32[256,256]{0,1:T(8,128)S(1)}, u32[]{:S(2)}, u32[]{:S(2)}) collective-permute-start(f32[256,256]{0,1:T(8,128)S(1)} %fusion.106), channel_id=1, source_target_pairs={{0,64},{64,0},{32,96},{96,32},{128,192},{192,128},{160,224},{224,1... | collective-permute-start | bytes 786440 | tf_op jit(solution)/shard_map/ppermute | solution.py:17
  760.1 10.1 %collective-permute-start.14 = (f32[256,256]{0,1:T(8,128)S(1)}, f32[256,256]{0,1:T(8,128)S(1)}, u32[]{:S(2)}, u32[]{:S(2)}) collective-permute-start(f32[256,256]{0,1:T(8,128)S(1)} %add.390), channel_id=1, source_target_pairs={{0,128},{128,0},{32,160},{160,32},{64,192},{192,64},{96,224},{224,... | collective-permute-start | bytes 786440 | tf_op jit(solution)/shard_map/ppermute | solution.py:17
  770.3 10.8 %collective-permute-start.15 = (f32[256,256]{0,1:T(8,128)S(1)}, f32[256,256]{0,1:T(8,128)S(1)}, u32[]{:S(2)}, u32[]{:S(2)}) collective-permute-start(f32[256,256]{0,1:T(8,128)S(1)} %add.391), channel_id=1, source_target_pairs={{0,256},{256,0},{32,288},{288,32},{64,320},{320,64},{96,352},{352,... | collective-permute-start | bytes 786440 | tf_op jit(solution)/shard_map/ppermute | solution.py:17
  843.6 104.0 %all-gather.20.cloned.1.call-start = ((), (), s32[]{:S(2)}) async-start(), calls=%async_computation.5 | async-start | bytes 2359296 | tf_op jit(solution)/shard_map/all_gather | solution.py:23
  949.7 3.2 collective-permute-start.16
  952.9 20.1 %collective-permute-start.17 = (bf16[1,256,256]{2,1,0:T(8,128)(2,1)S(1)}, bf16[1,256,256]{2,1,0:T(8,128)(2,1)S(1)}, u32[]{:S(2)}, u32[]{:S(2)}) collective-permute-start(bf16[1,256,256]{2,1,0:T(8,128)(2,1)S(1)} %fusion.105), channel_id=1, source_target_pairs={{0,64},{64,0},{32,96},{96,32},{128,192},{192,128},{160,224},{224,1... | collective-permute-start | bytes 393224 | tf_op jit(solution)/shard_map/ppermute | solution.py:17
  973.1 7.3 collective-permute-start.18
  980.4 8.4 collective-permute-start.19
  (1 other events, 3.8 us)
Sparse Core Ops, SparseCore 0:
  99.6 73.0 all-gather.9
  177.1 182.3 all-gather.15
  530.2 36.2 all-gather.11
  569.6 103.6 all-gather.17
  843.7 30.6 all-gather.13
  876.9 70.6 all-gather.19
